TPU v7x, 256 devices: a whole 4x4x8 slice. The times are simulated.
256 devices in a mesh: seq: 16 (over y, x), chan: 16 (over z, core).
Axes of the slice: x: 4, y: 4, z: 8, core: 2. Of those that a mesh axis runs over, the one named last changes fastest.
Arguments:
- tokens: bfloat16 [57344, 2048], P('seq', 'chan'), may hold values from -6 to 6
- w_query: bfloat16 [2048, 256], replicated, may hold values from -0.125 to 0.125
- w_key: bfloat16 [2048, 256], replicated, may hold values from -0.125 to 0.125
- w_value: bfloat16 [2048, 2048], P(None, 'chan'), may hold values from -0.125 to 0.125
- w_out: bfloat16 [2048, 2048], replicated, may hold values from -0.125 to 0.125
- gain: float32 [2048], replicated, may hold values from 0.1 to 1.9
Outputs:
- mixed: bfloat16 [57344, 2048], P('seq', 'chan')
All inputs are finite; a program needn't handle non-finite values.
Results may differ from a plain program's by a relative error of at most 0.019.
Values may be sent and summed in bfloat16 or wider, within the bound.
A program may use at most 128 MiB of HBM per device.

v0:
```python
import jax
import jax.numpy as jnp
from jax import lax
from jax.sharding import PartitionSpec as P

HEADS = 16
FEAT = 16
HEAD_DIM = 128
BLOCK = 896


def feature_parts(rows):
    linear = rows * FEAT ** (-0.25)
    square = (rows[..., :, None] * rows[..., None, :]).reshape(rows.shape[:-1] + (FEAT * FEAT,)) * (
        2.0 * FEAT
    ) ** (-0.5)
    return (linear, square)


def per_device(tokens, w_query, w_key, w_value, w_out, gain):
    highest = lax.Precision.HIGHEST
    groups = lax.axis_size("chan")
    per_group = HEADS // groups
    my_group = lax.axis_index("chan")
    my_slab = lax.axis_index("seq")
    tok_rows = tokens.shape[0]
    query_cols = per_group * FEAT
    value_cols = per_group * HEAD_DIM
    query_mine = lax.dynamic_slice_in_dim(w_query, my_group * query_cols, query_cols, 1)
    key_mine = lax.dynamic_slice_in_dim(w_key, my_group * query_cols, query_cols, 1)
    initial = (
        jnp.zeros((tok_rows, query_cols), jnp.float32),
        jnp.zeros((tok_rows, query_cols), jnp.float32),
        jnp.zeros((tok_rows, value_cols), jnp.float32),
    )
    piece = lax.all_gather(tokens, "chan", axis=1, tiled=True)
    query_sum, key_sum, value_sum = tuple(
        (
            jnp.dot(piece, weight, preferred_element_type=jnp.float32)
            for weight in (query_mine, key_mine, w_value)
        )
    )
    query_rows = query_sum.astype(jnp.bfloat16)
    key_rows = key_sum.astype(jnp.bfloat16)
    value_rows = value_sum.astype(jnp.bfloat16)
    blocks = tok_rows // BLOCK
    query_blocks = query_rows.reshape(blocks, BLOCK, per_group, FEAT)
    key_blocks = key_rows.reshape(blocks, BLOCK, per_group, FEAT)
    value_blocks = value_rows.reshape(blocks, BLOCK, per_group, HEAD_DIM)
    value_f32 = value_blocks.astype(jnp.float32)
    key_linear, key_square = feature_parts(key_blocks.astype(jnp.float32))
    own_zero = jnp.sum(value_f32, axis=1)
    own_one = jnp.einsum("bthf,bthe->bhfe", key_linear, value_f32, precision=highest)
    own_two = jnp.einsum("bthf,bthe->bhfe", key_square, value_f32, precision=highest)
    own = (own_zero, own_one, own_two)
    slab_total = tuple((jnp.sum(member, axis=0) for member in own))
    initial = tuple((jnp.zeros_like(member) for member in slab_total))
    pieces = (
        lax.all_gather(slab_total[0][None].astype(jnp.bfloat16), "seq", axis=0, tiled=True).astype(
            jnp.float32
        ),
        lax.all_gather(slab_total[1][None].astype(jnp.bfloat16), "seq", axis=0, tiled=True).astype(
            jnp.float32
        ),
        lax.all_gather(slab_total[2][None].astype(jnp.bfloat16), "seq", axis=0, tiled=True).astype(
            jnp.float32
        ),
    )
    count = pieces[0].shape[0]
    order = jnp.arange(count, dtype=jnp.int32)
    earlier_mask = order < my_slab
    prefix = tuple(
        (
            total
            + jnp.sum(
                jnp.where(earlier_mask.reshape((count,) + (1,) * (piece.ndim - 1)), piece, 0.0),
                axis=0,
            )
            for total, piece in zip(initial, pieces)
        )
    )
    earlier = tuple(
        (
            jnp.concatenate([jnp.zeros_like(member[:1]), jnp.cumsum(member, axis=0)[:-1]], axis=0)
            + base[None]
            for member, base in zip(own, prefix)
        )
    )
    query_linear, query_square = feature_parts(query_blocks.astype(jnp.float32))
    inter = earlier[0][:, None] + jnp.einsum(
        "bthf,bhfe->bthe", query_linear, earlier[1], precision=highest
    )
    inter = inter + jnp.einsum("bthf,bhfe->bthe", query_square, earlier[2], precision=highest)
    scores = jnp.einsum(
        "bthf,bshf->bhts", query_blocks, key_blocks, preferred_element_type=jnp.float32
    ) * FEAT ** (-0.5)
    kernel = 1.0 + scores + 0.5 * scores * scores
    causal = jnp.arange(BLOCK)[:, None] >= jnp.arange(BLOCK)[None, :]
    weights = jnp.where(causal, kernel, 0.0).astype(jnp.bfloat16)
    intra = jnp.einsum("bhts,bshe->bthe", weights, value_blocks, preferred_element_type=jnp.float32)
    numerator = (intra + inter).reshape(tok_rows, per_group, HEAD_DIM)
    gain_mine = lax.dynamic_slice_in_dim(gain, my_group * value_cols, value_cols, 0).reshape(
        per_group, HEAD_DIM
    )
    mean_square = jnp.mean(numerator * numerator, axis=-1, keepdims=True)
    hidden = (
        (numerator * lax.rsqrt(mean_square + 1e-05) * gain_mine)
        .astype(jnp.bfloat16)
        .reshape(tok_rows, value_cols)
    )
    out_mine = lax.dynamic_slice_in_dim(w_out, my_group * value_cols, value_cols, 0)
    partial_value = jnp.dot(hidden, out_mine, preferred_element_type=jnp.float32)
    partial_value = lax.optimization_barrier(partial_value.astype(jnp.bfloat16)).astype(jnp.float32)
    mixed = lax.psum_scatter(
        partial_value.astype(jnp.bfloat16), "chan", scatter_dimension=1, tiled=True
    )
    return mixed


def solution(mesh):
    return jax.shard_map(
        per_device,
        mesh=mesh,
        in_specs=(P("seq", "chan"), P(), P(), P(None, "chan"), P(), P()),
        out_specs=P("seq", "chan"),
        check_vma=False,
    )
```

profile of v0, /device:TPU:2, one launch (start us, length us, event | category | flops | bytes accessed | tf_op | source)
XLA Modules:
  0.0 357.5 jit_solution(1797674125439511556)
XLA Ops:
  6.5 0.7 all-gather.7.cloned.1.call-update
  7.3 0.0 all-gather.9.cloned.1.call-start
  7.3 0.8 dynamic_slice.14
  8.1 0.2 iota_compare_fusion
  8.3 96.7 %all-gather.7.cloned.1.call-done = bf16[3584,2048]{1,0:T(8,128)(2,1)} async-done(((bf16[3584,128]{1,0:T(8,128)(2,1)}), bf16[3584,2048]{1,0:T(8,128)(2,1)}) %all-gather.7.cloned.1.call-update) | async-done | bytes 14680080 | tf_op jit(solution)/shard_map/all_gather | solution.py:36
  105.0 9.2 %fusion.51 = (bf16[128]{0:T(256)(128)(2,1)S(1)}, bf16[3584,128]{1,0:T(8,128)(2,1)S(1)}) fusion(bf16[3584,2048]{1,0:T(8,128)(2,1)} %all-gather.7.cloned.1.call-done, bf16[2048,128]{1,0:T(8,128)(2,1)} %param.9), kind=kOutput, calls=%fused_computation.68 | convolution fusion | flops 1879965568 | bytes 16122112 | tf_op jit(solution)/shard_map/dot_general | solution.py:39
  114.3 0.1 convert_reduce_fusion
  114.4 9.4 %convolution_convert_fusion.2 = bf16[16,3584]{1,0:T(8,128)(2,1)S(1)} fusion(bf16[3584,2048]{1,0:T(8,128)(2,1)} %all-gather.7.cloned.1.call-done, bf16[2048,256]{1,0:T(8,128)(2,1)S(1)} %copy-done, s32[]{:T(128)S(6)} %select_n.25), kind=kOutput, calls=%fused_computation.3 | convolution fusion | flops 234938368 | bytes 15319044 | tf_op jit(solution)/shard_map/dot_general | solution.py:39
  123.8 0.5 fusion.50
  124.4 20.3 %all-gather.3 = bf16[16,1,128]{2,1,0:T(2,128)(2,1)S(1)} all-gather(bf16[1,1,128]{2,1,0:T(2,128)(2,1)S(1)} %bitcast.100), channel_id=2, replica_groups=mesh['seq'=16,'chan'=16] {'seq'}, dimensions={0}, use_global_device_ids=true | all-gather | bytes 4352 | tf_op jit(solution)/shard_map/all_gather | solution.py:59
  144.7 0.1 fusion.32
  144.8 21.4 %all-gather.1 = bf16[256,128]{1,0:T(8,128)(2,1)S(1)} all-gather(bf16[16,128]{1,0:T(8,128)(2,1)S(1)} %get-tuple-element.7), channel_id=3, replica_groups=mesh['seq'=16,'chan'=16] {'seq'}, dimensions={0}, use_global_device_ids=true | all-gather | bytes 69632 | tf_op jit(solution)/shard_map/all_gather | solution.py:62
  166.2 0.4 multiply_multiply_fusion.1
  166.6 2.5 fusion.49
  169.0 0.0 all-gather.9.cloned.1.call-update
  169.1 0.0 reduce-scatter.4.cloned.1.call-start
  169.1 0.4 fusion.8
  169.6 0.1 fusion.20
  169.7 0.1 fusion.37
  169.8 9.6 %convolution_convert_fusion.3 = bf16[16,3584]{1,0:T(8,128)(2,1)S(1)} fusion(bf16[3584,2048]{1,0:T(8,128)(2,1)} %all-gather.7.cloned.1.call-done, bf16[2048,256]{1,0:T(8,128)(2,1)} %param.7, s32[]{:T(128)S(6)} %select_n.25), kind=kOutput, calls=%fused_computation.4 | convolution fusion | flops 234938368 | bytes 15319044 | tf_op jit(solution)/shard_map/dot_general | solution.py:39
  179.4 2.9 fusion.16
  182.3 2.2 multiply_multiply_fusion
  184.5 29.4 %all-gather.9.cloned.1.call-done = bf16[4096,128]{1,0:T(8,128)(2,1)} async-done(((bf16[256,128]{1,0:T(8,128)(2,1)}), bf16[4096,128]{1,0:T(8,128)(2,1)}) %all-gather.9.cloned.1.call-update) | async-done | bytes 1048592 | tf_op jit(solution)/shard_map/all_gather | solution.py:65
  213.9 1.5 fusion
  215.4 5.6 %fusion.6 = f32[4,128,896]{2,1,0:T(8,128)} fusion(f32[4,896,256]{1,2,0:T(8,128)} %bitcast.84, f32[3,1,256,128]{3,2,0,1:T(8,128)S(1)} %slice-done, f32[256,128]{1,0:T(8,128)S(1)} %fusion), kind=kOutput, calls=%fused_computation.20 | convolution fusion | flops 1409417216 | bytes 6029312 | tf_op jit(solution)/shard_map/bthf,bhfe->bthe/dot_general | solution.py:93
  221.0 8.5 %multiply_reduce_fusion = (f32[4,896]{1,0:T(4,128)S(1)}, f32[4,896,1,128]{1,3,0,2:T(8,128)}) fusion(f32[4,128,896]{2,1,0:T(8,128)} %fusion.6, f32[4,128,896]{2,1,0:T(8,128)} %fusion.16, f32[4,128]{1,0:T(4,128)S(1)} %add_bitcast_fusion, bf16[4,896,128]{2,1,0:T(8,128)(2,1)S(1)} %bitcast.88, pred[896,896]{1,0:T(8,128)(4,1)S(1)} %iota_compare_fusion, ...), kind=kOutput, calls=%fused_computation.18 | convolution fusion | flops 949613056 | bytes 7471104 | tf_op jit(solution)/shard_map/bhts,bshe->bthe/dot_general | solution.py:100
  229.5 1.8 copy.41
  231.3 0.5 fusion.3
  231.9 8.3 %convolution_convert_fusion = bf16[3584,2048]{1,0:T(8,128)(2,1)} fusion(bf16[3584,128]{1,0:T(8,128)(2,1)S(1)} %fusion.3, bf16[2048,2048]{1,0:T(8,128)(2,1)} %param.10, s32[]{:T(128)S(6)} %select_n.30), kind=kOutput, calls=%fused_computation | convolution fusion | flops 1886388224 | bytes 16121860 | tf_op jit(solution)/shard_map/dot_general | solution.py:112
  240.2 18.8 %copy.45 = bf16[3584,2048]{0,1:T(8,128)(2,1)} copy(bf16[3584,2048]{1,0:T(8,128)(2,1)} %convolution_convert_fusion) | data formatting | bytes 29360128
  259.0 89.8 %reduce-scatter.4.cloned.1.call-done = bf16[128,3584]{1,0:T(8,128)(2,1)} async-done(((bf16[2048,3584]{1,0:T(8,128)(2,1)}), bf16[128,3584]{1,0:T(8,128)(2,1)}) %reduce-scatter.4.cloned.1.call-update) | async-done | bytes 917520
  348.8 2.2 copy.46
  (21 shorter events, 0.2 us)
Async XLA Ops:
  6.5 107.9 %copy-start = (bf16[2048,256]{1,0:T(8,128)(2,1)S(1)}, bf16[2048,256]{1,0:T(8,128)(2,1)}, u32[]{:S(2)}) copy-start(bf16[2048,256]{1,0:T(8,128)(2,1)} %param.8) | copy-start | bytes 3145732
  6.5 98.5 %all-gather.7.cloned.1.call-start = ((), (), s32[]{:S(2)}) async-start(), calls=%async_computation.1 | async-start | bytes 15597568 | tf_op jit(solution)/shard_map/all_gather | solution.py:36
  7.3 206.7 %all-gather.9.cloned.1.call-start = ((), (), s32[]{:S(2)}) async-start(), calls=%async_computation.2 | async-start | bytes 1114112 | tf_op jit(solution)/shard_map/all_gather | solution.py:65
  144.8 24.3 %copy-start.3 = (f32[4,1,16,128]{3,2,0,1:T(8,128)}, f32[4,1,16,128]{3,2,0,1:T(8,128)S(1)}, u32[]{:S(2)}) copy-start(f32[4,1,16,128]{3,2,0,1:T(8,128)S(1)} %fusion.32) | copy-start | bytes 98308
  169.1 179.7 %reduce-scatter.4.cloned.1.call-start = ((), (), s32[]{:S(2)}) async-start(), calls=%async_computation.3 | async-start | bytes 15597568
  169.5 9.9 %copy-start.2 = (f32[4,1,256,128]{3,2,0,1:T(8,128)}, f32[4,1,256,128]{3,2,0,1:T(8,128)S(1)}, u32[]{:S(2)}) copy-start(f32[4,1,256,128]{3,2,0,1:T(8,128)S(1)} %fusion.8) | copy-start | bytes 1572868
  169.8 9.6 %slice-start.1 = ((f32[4,1,16,128]{3,2,0,1:T(8,128)}), f32[3,1,16,128]{3,2,0,1:T(8,128)S(1)}, s32[]{:S(2)}) async-start(f32[4,1,16,128]{3,2,0,1:T(8,128)} %copy-done.3), calls=%async_computation.5 | async-start | bytes 49152 | tf_op jit(solution)/shard_map/slice | solution.py:84
  179.4 36.0 %slice-start = ((f32[4,1,256,128]{3,2,0,1:T(8,128)}), f32[3,1,256,128]{3,2,0,1:T(8,128)S(1)}, s32[]{:S(2)}) async-start(f32[4,1,256,128]{3,2,0,1:T(8,128)} %copy-done.2), calls=%async_computation.4 | async-start | bytes 786432 | tf_op jit(solution)/shard_map/slice | solution.py:84
  259.0 92.0 %copy-start.1 = (bf16[2048,256]{1,0:T(8,128)(2,1)S(1)}, bf16[2048,256]{1,0:T(8,128)(2,1)}, u32[]{:S(2)}) copy-start(bf16[2048,256]{1,0:T(8,128)(2,1)} %param.8) | copy-start | bytes 3145732
Sparse Core Ops, SparseCore 0:
  9.1 95.8 all-gather.6
  169.2 44.6 all-gather.8
  259.1 89.6 reduce-scatter.3
where the time goes:
time: 358 us
  waiting for transfers between devices  217 us (61%)
  matrix products  56.4 us (16%)
  blocking collectives  41.7 us (12%)
  local copies, waits for them, and re-layouts  23.6 us (7%)
  between operations  13.3 us (4%)
  other arithmetic  5.75 us (2%)
    all_gather x1, waiting for transfers between devices, per_device(): piece = lax.all_gather(tokens, 'chan', axis=1, tiled=True)  96.7 us
    unnamed x4, waiting for transfers between devices  90.5 us
    all_gather x1, waiting for transfers between devices, per_device(): lax.all_gather(slab_total[2][None].astype(jnp.bfloat16), 'seq', axis=0, t...  29.4 us
    dot_general x3, matrix products, per_device(): jnp.dot(piece, weight, preferred_element_type=jnp.float32)  28.2 us
    all_gather x1, blocking collectives, per_device(): lax.all_gather(slab_total[1][None].astype(jnp.bfloat16), 'seq', axis=0, t...  21.4 us
    unnamed x10, local copies, waits for them, and re-layouts  21 us
    all_gather x1, blocking collectives, per_device(): lax.all_gather(slab_total[0][None].astype(jnp.bfloat16), 'seq', axis=0, t...  20.3 us
    dot_general x1, matrix products, per_device(): jnp.einsum('bhts,bshe->bthe', weights, value_blocks, preferred_element_ty...  8.45 us
  transfers between devices with their start and end apart: 3, of which 3 were waited for; matrix products, arithmetic and copies ran while one was open for 5% of the time, Pallas kernels for 0%

commit v1 on v0

--- a/solution.py
+++ b/solution.py
@@ -33,7 +33,14 @@
         jnp.zeros((tok_rows, query_cols), jnp.float32),
         jnp.zeros((tok_rows, value_cols), jnp.float32),
     )
-    piece = lax.all_gather(tokens, "chan", axis=1, tiled=True)
+    slots = lax.psum(1, "chan")
+    tray = tuple(((s, (s + 1) % slots) for s in range(slots)))
+    local_out = [None] * slots
+    local_out[slots - 1] = tokens
+    for rr in range(slots - 2, -1, -1):
+        local_out[rr] = lax.ppermute(local_out[rr + 1], "chan", perm=tray)
+    s_next = jnp.concatenate(local_out, axis=1)
+    piece = jnp.roll(s_next, (lax.axis_index("chan") + 1) * tokens.shape[1], 1)
     query_sum, key_sum, value_sum = tuple(
         (
             jnp.dot(piece, weight, preferred_element_type=jnp.float32)

time: 358 us -> 507 us (1.42)
  waiting for transfers between devices: 217 us -> 300 us
  local copies, waits for them, and re-layouts: 23.6 us -> 88.9 us
    ppermute x0 -> x15, waiting for transfers between devices: none -> 211 us  [per_device(): local_out[rr] = lax.ppermute(local_out[rr + 1], 'chan', perm=tray)]
    all_gather x1 -> x0, waiting for transfers between devices: 96.7 us -> none  [per_device(): piece = lax.all_gather(tokens, 'chan', axis=1, tiled=True)]
    unnamed x10 -> x87, local copies, waits for them, and re-layouts: 21 us -> 85.1 us
    all_gather x1, waiting for transfers between devices: 29.4 us -> 0.01 us  [per_device(): lax.all_gather(slab_total[2][None].astype(jnp.bfloat16), 'seq', axis=0, t...]
    unnamed x4 -> x3, waiting for transfers between devices: 90.5 us -> 89 us
  transfers between devices with their start and end apart: 3 -> 17, of which waited for: 3 -> 16; matrix products, arithmetic and copies ran while one was open for 5% -> 3% of each run, Pallas kernels for 0% -> 0%
where the time goes in v1:
time: 507 us; the launch traced here: 506 us
  waiting for transfers between devices  300 us (59%)
  local copies, waits for them, and re-layouts  88.9 us (18%)
  matrix products  54.3 us (11%)
  blocking collectives  42.2 us (8%)
  between operations  13.7 us (3%)
  other arithmetic  6.54 us (1%)
    ppermute x15, waiting for transfers between devices, per_device(): local_out[rr] = lax.ppermute(local_out[rr + 1], 'chan', perm=tray)  211 us
    unnamed x3, waiting for transfers between devices  89 us
    unnamed x87, local copies, waits for them, and re-layouts  85.1 us
    dot_general x3, matrix products, per_device(): jnp.dot(piece, weight, preferred_element_type=jnp.float32)  26.2 us
    all_gather x1, blocking collectives, per_device(): lax.all_gather(slab_total[1][None].astype(jnp.bfloat16), 'seq', axis=0, t...  21.6 us
    all_gather x1, blocking collectives, per_device(): lax.all_gather(slab_total[0][None].astype(jnp.bfloat16), 'seq', axis=0, t...  20.6 us
  transfers between devices with their start and end apart: 17, of which 16 were waited for; matrix products, arithmetic and copies ran while one was open for 3% of the time, Pallas kernels for 0%

profile of v1, /device:TPU:2, one launch (start us, length us, event | category | flops | bytes accessed | tf_op | source)
XLA Modules:
  0.0 505.9 jit_solution(1647778096592941649)
XLA Ops:
  6.6 16.6 %collective-permute-done = bf16[3584,128]{1,0:T(8,128)(2,1)S(1)} collective-permute-done((bf16[3584,128]{1,0:T(8,128)(2,1)}, bf16[3584,128]{1,0:T(8,128)(2,1)S(1)}, u32[]{:S(2)}, u32[]{:S(2)}) %collective-permute-start) | collective-permute-done | bytes 917536 | tf_op jit(solution)/shard_map/ppermute | solution.py:41
  23.2 14.0 %collective-permute-done.1 = bf16[3584,128]{1,0:T(8,128)(2,1)S(1)} collective-permute-done((bf16[3584,128]{1,0:T(8,128)(2,1)S(1)}, bf16[3584,128]{1,0:T(8,128)(2,1)S(1)}, u32[]{:S(2)}, u32[]{:S(2)}) %collective-permute-start.1) | collective-permute-done | bytes 917536 | tf_op jit(solution)/shard_map/ppermute | solution.py:41
  38.2 14.0 %collective-permute-done.2 = bf16[3584,128]{1,0:T(8,128)(2,1)S(1)} collective-permute-done((bf16[3584,128]{1,0:T(8,128)(2,1)S(1)}, bf16[3584,128]{1,0:T(8,128)(2,1)S(1)}, u32[]{:S(2)}, u32[]{:S(2)}) %collective-permute-start.2) | collective-permute-done | bytes 917536 | tf_op jit(solution)/shard_map/ppermute | solution.py:41
  53.1 14.0 %collective-permute-done.3 = bf16[3584,128]{1,0:T(8,128)(2,1)S(1)} collective-permute-done((bf16[3584,128]{1,0:T(8,128)(2,1)S(1)}, bf16[3584,128]{1,0:T(8,128)(2,1)S(1)}, u32[]{:S(2)}, u32[]{:S(2)}) %collective-permute-start.3) | collective-permute-done | bytes 917536 | tf_op jit(solution)/shard_map/ppermute | solution.py:41
  68.1 14.0 %collective-permute-done.4 = bf16[3584,128]{1,0:T(8,128)(2,1)S(1)} collective-permute-done((bf16[3584,128]{1,0:T(8,128)(2,1)S(1)}, bf16[3584,128]{1,0:T(8,128)(2,1)S(1)}, u32[]{:S(2)}, u32[]{:S(2)}) %collective-permute-start.4) | collective-permute-done | bytes 917536 | tf_op jit(solution)/shard_map/ppermute | solution.py:41
  83.1 14.0 %collective-permute-done.5 = bf16[3584,128]{1,0:T(8,128)(2,1)S(1)} collective-permute-done((bf16[3584,128]{1,0:T(8,128)(2,1)S(1)}, bf16[3584,128]{1,0:T(8,128)(2,1)S(1)}, u32[]{:S(2)}, u32[]{:S(2)}) %collective-permute-start.5) | collective-permute-done | bytes 917536 | tf_op jit(solution)/shard_map/ppermute | solution.py:41
  98.1 14.0 %collective-permute-done.6 = bf16[3584,128]{1,0:T(8,128)(2,1)S(1)} collective-permute-done((bf16[3584,128]{1,0:T(8,128)(2,1)S(1)}, bf16[3584,128]{1,0:T(8,128)(2,1)S(1)}, u32[]{:S(2)}, u32[]{:S(2)}) %collective-permute-start.6) | collective-permute-done | bytes 917536 | tf_op jit(solution)/shard_map/ppermute | solution.py:41
  113.0 14.0 %collective-permute-done.7 = bf16[3584,128]{1,0:T(8,128)(2,1)S(1)} collective-permute-done((bf16[3584,128]{1,0:T(8,128)(2,1)S(1)}, bf16[3584,128]{1,0:T(8,128)(2,1)S(1)}, u32[]{:S(2)}, u32[]{:S(2)}) %collective-permute-start.7) | collective-permute-done | bytes 917536 | tf_op jit(solution)/shard_map/ppermute | solution.py:41
  128.0 14.0 %collective-permute-done.8 = bf16[3584,128]{1,0:T(8,128)(2,1)S(1)} collective-permute-done((bf16[3584,128]{1,0:T(8,128)(2,1)S(1)}, bf16[3584,128]{1,0:T(8,128)(2,1)S(1)}, u32[]{:S(2)}, u32[]{:S(2)}) %collective-permute-start.8) | collective-permute-done | bytes 917536 | tf_op jit(solution)/shard_map/ppermute | solution.py:41
  143.0 14.0 %collective-permute-done.9 = bf16[3584,128]{1,0:T(8,128)(2,1)S(1)} collective-permute-done((bf16[3584,128]{1,0:T(8,128)(2,1)S(1)}, bf16[3584,128]{1,0:T(8,128)(2,1)S(1)}, u32[]{:S(2)}, u32[]{:S(2)}) %collective-permute-start.9) | collective-permute-done | bytes 917536 | tf_op jit(solution)/shard_map/ppermute | solution.py:41
  158.0 14.0 %collective-permute-done.10 = bf16[3584,128]{1,0:T(8,128)(2,1)S(1)} collective-permute-done((bf16[3584,128]{1,0:T(8,128)(2,1)S(1)}, bf16[3584,128]{1,0:T(8,128)(2,1)S(1)}, u32[]{:S(2)}, u32[]{:S(2)}) %collective-permute-start.10) | collective-permute-done | bytes 917536 | tf_op jit(solution)/shard_map/ppermute | solution.py:41
  172.9 14.0 %collective-permute-done.11 = bf16[3584,128]{1,0:T(8,128)(2,1)S(1)} collective-permute-done((bf16[3584,128]{1,0:T(8,128)(2,1)S(1)}, bf16[3584,128]{1,0:T(8,128)(2,1)S(1)}, u32[]{:S(2)}, u32[]{:S(2)}) %collective-permute-start.11) | collective-permute-done | bytes 917536 | tf_op jit(solution)/shard_map/ppermute | solution.py:41
  187.9 14.0 %collective-permute-done.12 = bf16[3584,128]{1,0:T(8,128)(2,1)S(1)} collective-permute-done((bf16[3584,128]{1,0:T(8,128)(2,1)S(1)}, bf16[3584,128]{1,0:T(8,128)(2,1)S(1)}, u32[]{:S(2)}, u32[]{:S(2)}) %collective-permute-start.12) | collective-permute-done | bytes 917536 | tf_op jit(solution)/shard_map/ppermute | solution.py:41
  202.9 14.1 %collective-permute-done.13 = bf16[3584,128]{1,0:T(8,128)(2,1)} collective-permute-done((bf16[3584,128]{1,0:T(8,128)(2,1)S(1)}, bf16[3584,128]{1,0:T(8,128)(2,1)}, u32[]{:S(2)}, u32[]{:S(2)}) %collective-permute-start.13) | collective-permute-done | bytes 917536 | tf_op jit(solution)/shard_map/ppermute | solution.py:41
  219.2 12.1 %collective-permute-done.14 = bf16[3584,128]{1,0:T(8,128)(2,1)} collective-permute-done((bf16[3584,128]{1,0:T(8,128)(2,1)}, bf16[3584,128]{1,0:T(8,128)(2,1)}, u32[]{:S(2)}, u32[]{:S(2)}) %collective-permute-start.14) | collective-permute-done | bytes 917536 | tf_op jit(solution)/shard_map/ppermute | solution.py:41
  240.2 2.3 constant_dynamic-update-slice_fusion.27
  249.0 2.2 constant_dynamic-update-slice_fusion.23
  253.5 2.3 constant_dynamic-update-slice_fusion.21
  260.3 2.2 constant_dynamic-update-slice_fusion.18
  265.8 2.3 constant_dynamic-update-slice_fusion.15
  285.2 7.8 %fusion.67 = (bf16[128]{0:T(256)(128)(2,1)S(1)}, bf16[3584,128]{1,0:T(8,128)(2,1)S(1)}) fusion(bf16[2048,128]{1,0:T(8,128)(2,1)S(1)} %copy-done.26, bf16[3584,4096]{1,0:T(8,128)(2,1)} %constant_dynamic-update-slice_fusion, s32[]{:T(128)S(6)} %select_n.39), kind=kOutput, calls=%fused_computation.107 | convolution fusion | flops 1879965568 | bytes 16122116 | tf_op jit(solution)/shard_map/dot_general | solution.py:46
  293.0 9.1 %fusion.12 = bf16[3584,16]{0,1:T(8,128)(2,1)S(1)} fusion(bf16[3584,4096]{1,0:T(8,128)(2,1)} %constant_dynamic-update-slice_fusion, s32[]{:T(128)S(6)} %select_n.39, bf16[2048,256]{1,0:T(8,128)(2,1)S(1)} %copy-done, s32[]{:T(128)S(6)} %select_n.40), kind=kOutput, calls=%fused_computation.10 | convolution fusion | flops 234938368 | bytes 15319048 | tf_op jit(solution)/shard_map/dot_general | solution.py:46
  303.2 2.5 fusion.65
  306.2 20.6 %all-gather.3 = bf16[16,1,128]{2,1,0:T(2,128)(2,1)S(1)} all-gather(bf16[1,1,128]{2,1,0:T(2,128)(2,1)S(1)} %bitcast.95), channel_id=2, replica_groups=mesh['seq'=16,'chan'=16] {'seq'}, dimensions={0}, use_global_device_ids=true | all-gather | bytes 4352 | tf_op jit(solution)/shard_map/all_gather | solution.py:66
  326.8 21.6 %all-gather.1 = bf16[256,128]{1,0:T(8,128)(2,1)S(1)} all-gather(bf16[16,128]{1,0:T(8,128)(2,1)S(1)} %get-tuple-element.7), channel_id=3, replica_groups=mesh['seq'=16,'chan'=16] {'seq'}, dimensions={0}, use_global_device_ids=true | all-gather | bytes 69632 | tf_op jit(solution)/shard_map/all_gather | solution.py:69
  348.6 9.3 %fusion.9 = bf16[3584,16]{0,1:T(8,128)(2,1)S(1)} fusion(bf16[3584,4096]{1,0:T(8,128)(2,1)} %constant_dynamic-update-slice_fusion, s32[]{:T(128)S(6)} %select_n.39, bf16[2048,256]{1,0:T(8,128)(2,1)} %param.7, s32[]{:T(128)S(6)} %select_n.40), kind=kOutput, calls=%fused_computation.9 | convolution fusion | flops 234938368 | bytes 15319048 | tf_op jit(solution)/shard_map/dot_general | solution.py:46
  357.9 2.9 fusion.31
  364.5 5.5 %fusion.21 = f32[4,128,896]{2,1,0:T(8,128)} fusion(f32[4,896,256]{1,2,0:T(8,128)} %bitcast.79, f32[3,1,256,128]{3,2,0,1:T(8,128)S(1)} %slice.13, f32[256,128]{1,0:T(8,128)S(1)} %fusion.15), kind=kOutput, calls=%fused_computation.26 | convolution fusion | flops 1409417216 | bytes 6029312 | tf_op jit(solution)/shard_map/bthf,bhfe->bthe/dot_general | solution.py:100
  370.0 8.4 %multiply_reduce_fusion = (f32[4,896]{1,0:T(4,128)S(1)}, f32[4,896,1,128]{1,3,0,2:T(8,128)}) fusion(f32[4,128,896]{2,1,0:T(8,128)} %fusion.21, f32[4,128,896]{2,1,0:T(8,128)} %fusion.31, f32[4,128]{1,0:T(4,128)S(1)} %add_bitcast_fusion, bf16[4,896,128]{2,1,0:T(8,128)(2,1)S(1)} %bitcast.83, pred[896,896]{1,0:T(8,128)(4,1)} %iota_compare_fusion, ...), kind=kOutput, calls=%fused_computation.24 | convolution fusion | flops 949613056 | bytes 7471104 | tf_op jit(solution)/shard_map/bhts,bshe->bthe/dot_general | solution.py:107
  380.8 8.3 %convolution_convert_fusion = bf16[3584,2048]{1,0:T(8,128)(2,1)} fusion(bf16[3584,128]{1,0:T(8,128)(2,1)S(1)} %fusion.18, bf16[2048,2048]{1,0:T(8,128)(2,1)} %param.10, s32[]{:T(128)S(6)} %select_n.45), kind=kOutput, calls=%fused_computation | convolution fusion | flops 1886388224 | bytes 16121860 | tf_op jit(solution)/shard_map/dot_general | solution.py:119
  389.1 18.8 %copy.45 = bf16[3584,2048]{0,1:T(8,128)(2,1)} copy(bf16[3584,2048]{1,0:T(8,128)(2,1)} %convolution_convert_fusion) | data formatting | bytes 29360128
  407.9 89.0 %reduce-scatter.4.cloned.1.call-done = bf16[128,3584]{1,0:T(8,128)(2,1)} async-done(((bf16[2048,3584]{1,0:T(8,128)(2,1)}), bf16[128,3584]{1,0:T(8,128)(2,1)}) %reduce-scatter.4.cloned.1.call-update) | async-done | bytes 917520
  (124 shorter events, 66.0 us)
Async XLA Ops:
  6.5 286.4 %copy-start = (bf16[2048,256]{1,0:T(8,128)(2,1)S(1)}, bf16[2048,256]{1,0:T(8,128)(2,1)}, u32[]{:S(2)}) copy-start(bf16[2048,256]{1,0:T(8,128)(2,1)} %param.8) | copy-start | bytes 3145732
  6.5 277.6 %copy-start.1 = (bf16[3584,128]{1,0:T(8,128)(2,1)S(1)}, bf16[3584,128]{1,0:T(8,128)(2,1)}, u32[]{:S(2)}) copy-start(bf16[3584,128]{1,0:T(8,128)(2,1)} %param.6) | copy-start | bytes 2752516
  6.5 356.4 %all-gather.6.cloned.1.call-start = ((), (), s32[]{:S(2)}) async-start(), calls=%async_computation.1 | async-start | bytes 1114112 | tf_op jit(solution)/shard_map/all_gather | solution.py:72
  6.5 16.6 %collective-permute-start = (bf16[3584,128]{1,0:T(8,128)(2,1)}, bf16[3584,128]{1,0:T(8,128)(2,1)S(1)}, u32[]{:S(2)}, u32[]{:S(2)}) collective-permute-start(bf16[3584,128]{1,0:T(8,128)(2,1)} %param.6), channel_id=1, source_target_pairs={{0,1},{1,2},{2,3},{3,4},{4,5},{5,6},{6,7},{7,8},{8,9},{9,10},{10,1... | collective-permute-start | bytes 2752520 | tf_op jit(solution)/shard_map/ppermute | solution.py:41
  23.2 14.0 %collective-permute-start.1 = (bf16[3584,128]{1,0:T(8,128)(2,1)S(1)}, bf16[3584,128]{1,0:T(8,128)(2,1)S(1)}, u32[]{:S(2)}, u32[]{:S(2)}) collective-permute-start(bf16[3584,128]{1,0:T(8,128)(2,1)S(1)} %collective-permute-done), channel_id=1, source_target_pairs={{0,1},{1,2},{2,3},{3,4},{4,5},{5,6},{6,7},{7,8},{8,9},{9,10},{10,1... | collective-permute-start | bytes 2752520 | tf_op jit(solution)/shard_map/ppermute | solution.py:41
  38.2 14.0 %collective-permute-start.2 = (bf16[3584,128]{1,0:T(8,128)(2,1)S(1)}, bf16[3584,128]{1,0:T(8,128)(2,1)S(1)}, u32[]{:S(2)}, u32[]{:S(2)}) collective-permute-start(bf16[3584,128]{1,0:T(8,128)(2,1)S(1)} %collective-permute-done.1), channel_id=1, source_target_pairs={{0,1},{1,2},{2,3},{3,4},{4,5},{5,6},{6,7},{7,8},{8,9},{9,10},{10,1... | collective-permute-start | bytes 2752520 | tf_op jit(solution)/shard_map/ppermute | solution.py:41
  53.1 14.0 %collective-permute-start.3 = (bf16[3584,128]{1,0:T(8,128)(2,1)S(1)}, bf16[3584,128]{1,0:T(8,128)(2,1)S(1)}, u32[]{:S(2)}, u32[]{:S(2)}) collective-permute-start(bf16[3584,128]{1,0:T(8,128)(2,1)S(1)} %collective-permute-done.2), channel_id=1, source_target_pairs={{0,1},{1,2},{2,3},{3,4},{4,5},{5,6},{6,7},{7,8},{8,9},{9,10},{10,1... | collective-permute-start | bytes 2752520 | tf_op jit(solution)/shard_map/ppermute | solution.py:41
  68.1 14.0 %collective-permute-start.4 = (bf16[3584,128]{1,0:T(8,128)(2,1)S(1)}, bf16[3584,128]{1,0:T(8,128)(2,1)S(1)}, u32[]{:S(2)}, u32[]{:S(2)}) collective-permute-start(bf16[3584,128]{1,0:T(8,128)(2,1)S(1)} %collective-permute-done.3), channel_id=1, source_target_pairs={{0,1},{1,2},{2,3},{3,4},{4,5},{5,6},{6,7},{7,8},{8,9},{9,10},{10,1... | collective-permute-start | bytes 2752520 | tf_op jit(solution)/shard_map/ppermute | solution.py:41
  83.1 14.0 %collective-permute-start.5 = (bf16[3584,128]{1,0:T(8,128)(2,1)S(1)}, bf16[3584,128]{1,0:T(8,128)(2,1)S(1)}, u32[]{:S(2)}, u32[]{:S(2)}) collective-permute-start(bf16[3584,128]{1,0:T(8,128)(2,1)S(1)} %collective-permute-done.4), channel_id=1, source_target_pairs={{0,1},{1,2},{2,3},{3,4},{4,5},{5,6},{6,7},{7,8},{8,9},{9,10},{10,1... | collective-permute-start | bytes 2752520 | tf_op jit(solution)/shard_map/ppermute | solution.py:41
  98.1 14.0 %collective-permute-start.6 = (bf16[3584,128]{1,0:T(8,128)(2,1)S(1)}, bf16[3584,128]{1,0:T(8,128)(2,1)S(1)}, u32[]{:S(2)}, u32[]{:S(2)}) collective-permute-start(bf16[3584,128]{1,0:T(8,128)(2,1)S(1)} %collective-permute-done.5), channel_id=1, source_target_pairs={{0,1},{1,2},{2,3},{3,4},{4,5},{5,6},{6,7},{7,8},{8,9},{9,10},{10,1... | collective-permute-start | bytes 2752520 | tf_op jit(solution)/shard_map/ppermute | solution.py:41
  113.0 14.0 %collective-permute-start.7 = (bf16[3584,128]{1,0:T(8,128)(2,1)S(1)}, bf16[3584,128]{1,0:T(8,128)(2,1)S(1)}, u32[]{:S(2)}, u32[]{:S(2)}) collective-permute-start(bf16[3584,128]{1,0:T(8,128)(2,1)S(1)} %collective-permute-done.6), channel_id=1, source_target_pairs={{0,1},{1,2},{2,3},{3,4},{4,5},{5,6},{6,7},{7,8},{8,9},{9,10},{10,1... | collective-permute-start | bytes 2752520 | tf_op jit(solution)/shard_map/ppermute | solution.py:41
  128.0 14.0 %collective-permute-start.8 = (bf16[3584,128]{1,0:T(8,128)(2,1)S(1)}, bf16[3584,128]{1,0:T(8,128)(2,1)S(1)}, u32[]{:S(2)}, u32[]{:S(2)}) collective-permute-start(bf16[3584,128]{1,0:T(8,128)(2,1)S(1)} %collective-permute-done.7), channel_id=1, source_target_pairs={{0,1},{1,2},{2,3},{3,4},{4,5},{5,6},{6,7},{7,8},{8,9},{9,10},{10,1... | collective-permute-start | bytes 2752520 | tf_op jit(solution)/shard_map/ppermute | solution.py:41
  142.9 14.0 %collective-permute-start.9 = (bf16[3584,128]{1,0:T(8,128)(2,1)S(1)}, bf16[3584,128]{1,0:T(8,128)(2,1)S(1)}, u32[]{:S(2)}, u32[]{:S(2)}) collective-permute-start(bf16[3584,128]{1,0:T(8,128)(2,1)S(1)} %collective-permute-done.8), channel_id=1, source_target_pairs={{0,1},{1,2},{2,3},{3,4},{4,5},{5,6},{6,7},{7,8},{8,9},{9,10},{10,1... | collective-permute-start | bytes 2752520 | tf_op jit(solution)/shard_map/ppermute | solution.py:41
  158.0 14.0 %collective-permute-start.10 = (bf16[3584,128]{1,0:T(8,128)(2,1)S(1)}, bf16[3584,128]{1,0:T(8,128)(2,1)S(1)}, u32[]{:S(2)}, u32[]{:S(2)}) collective-permute-start(bf16[3584,128]{1,0:T(8,128)(2,1)S(1)} %collective-permute-done.9), channel_id=1, source_target_pairs={{0,1},{1,2},{2,3},{3,4},{4,5},{5,6},{6,7},{7,8},{8,9},{9,10},{10,1... | collective-permute-start | bytes 2752520 | tf_op jit(solution)/shard_map/ppermute | solution.py:41
  172.9 14.0 %collective-permute-start.11 = (bf16[3584,128]{1,0:T(8,128)(2,1)S(1)}, bf16[3584,128]{1,0:T(8,128)(2,1)S(1)}, u32[]{:S(2)}, u32[]{:S(2)}) collective-permute-start(bf16[3584,128]{1,0:T(8,128)(2,1)S(1)} %collective-permute-done.10), channel_id=1, source_target_pairs={{0,1},{1,2},{2,3},{3,4},{4,5},{5,6},{6,7},{7,8},{8,9},{9,10},{10,1... | collective-permute-start | bytes 2752520 | tf_op jit(solution)/shard_map/ppermute | solution.py:41
  187.9 14.0 %collective-permute-start.12 = (bf16[3584,128]{1,0:T(8,128)(2,1)S(1)}, bf16[3584,128]{1,0:T(8,128)(2,1)S(1)}, u32[]{:S(2)}, u32[]{:S(2)}) collective-permute-start(bf16[3584,128]{1,0:T(8,128)(2,1)S(1)} %collective-permute-done.11), channel_id=1, source_target_pairs={{0,1},{1,2},{2,3},{3,4},{4,5},{5,6},{6,7},{7,8},{8,9},{9,10},{10,1... | collective-permute-start | bytes 2752520 | tf_op jit(solution)/shard_map/ppermute | solution.py:41
  202.9 14.1 %collective-permute-start.13 = (bf16[3584,128]{1,0:T(8,128)(2,1)S(1)}, bf16[3584,128]{1,0:T(8,128)(2,1)}, u32[]{:S(2)}, u32[]{:S(2)}) collective-permute-start(bf16[3584,128]{1,0:T(8,128)(2,1)S(1)} %collective-permute-done.12), channel_id=1, source_target_pairs={{0,1},{1,2},{2,3},{3,4},{4,5},{5,6},{6,7},{7,8},{8,9},{9,10},{10,1... | collective-permute-start | bytes 2752520 | tf_op jit(solution)/shard_map/ppermute | solution.py:41
  217.0 14.3 %collective-permute-start.14 = (bf16[3584,128]{1,0:T(8,128)(2,1)}, bf16[3584,128]{1,0:T(8,128)(2,1)}, u32[]{:S(2)}, u32[]{:S(2)}) collective-permute-start(bf16[3584,128]{1,0:T(8,128)(2,1)} %collective-permute-done.13), channel_id=1, source_target_pairs={{0,1},{1,2},{2,3},{3,4},{4,5},{5,6},{6,7},{7,8},{8,9},{9,10},{10,1... | collective-permute-start | bytes 2752520 | tf_op jit(solution)/shard_map/ppermute | solution.py:41
  217.0 53.3 %copy-start.25 = (bf16[3584,128]{1,0:T(8,128)(2,1)S(1)}, bf16[3584,128]{1,0:T(8,128)(2,1)}, u32[]{:S(2)}) copy-start(bf16[3584,128]{1,0:T(8,128)(2,1)} %copy-done.24) | copy-start | bytes 2752516
  217.0 54.4 %copy-start.23 = (bf16[3584,128]{1,0:T(8,128)(2,1)S(1)}, bf16[3584,128]{1,0:T(8,128)(2,1)}, u32[]{:S(2)}) copy-start(bf16[3584,128]{1,0:T(8,128)(2,1)} %copy-done.22) | copy-start | bytes 2752516
  217.0 55.5 %copy-start.21 = (bf16[3584,128]{1,0:T(8,128)(2,1)S(1)}, bf16[3584,128]{1,0:T(8,128)(2,1)}, u32[]{:S(2)}) copy-start(bf16[3584,128]{1,0:T(8,128)(2,1)} %copy-done.20) | copy-start | bytes 2752516
  217.0 56.5 %copy-start.19 = (bf16[3584,128]{1,0:T(8,128)(2,1)S(1)}, bf16[3584,128]{1,0:T(8,128)(2,1)}, u32[]{:S(2)}) copy-start(bf16[3584,128]{1,0:T(8,128)(2,1)} %copy-done.18) | copy-start | bytes 2752516
  217.0 57.6 %copy-start.17 = (bf16[3584,128]{1,0:T(8,128)(2,1)S(1)}, bf16[3584,128]{1,0:T(8,128)(2,1)}, u32[]{:S(2)}) copy-start(bf16[3584,128]{1,0:T(8,128)(2,1)} %copy-done.16) | copy-start | bytes 2752516
  217.0 58.6 %copy-start.15 = (bf16[3584,128]{1,0:T(8,128)(2,1)S(1)}, bf16[3584,128]{1,0:T(8,128)(2,1)}, u32[]{:S(2)}) copy-start(bf16[3584,128]{1,0:T(8,128)(2,1)} %copy-done.14) | copy-start | bytes 2752516
  217.0 59.8 %copy-start.13 = (bf16[3584,128]{1,0:T(8,128)(2,1)S(1)}, bf16[3584,128]{1,0:T(8,128)(2,1)}, u32[]{:S(2)}) copy-start(bf16[3584,128]{1,0:T(8,128)(2,1)} %copy-done.12) | copy-start | bytes 2752516
  217.0 60.8 %copy-start.11 = (bf16[3584,128]{1,0:T(8,128)(2,1)S(1)}, bf16[3584,128]{1,0:T(8,128)(2,1)}, u32[]{:S(2)}) copy-start(bf16[3584,128]{1,0:T(8,128)(2,1)} %copy-done.10) | copy-start | bytes 2752516
  217.1 61.8 %copy-start.9 = (bf16[3584,128]{1,0:T(8,128)(2,1)S(1)}, bf16[3584,128]{1,0:T(8,128)(2,1)}, u32[]{:S(2)}) copy-start(bf16[3584,128]{1,0:T(8,128)(2,1)} %copy-done.8) | copy-start | bytes 2752516
  217.1 62.8 %copy-start.7 = (bf16[3584,128]{1,0:T(8,128)(2,1)S(1)}, bf16[3584,128]{1,0:T(8,128)(2,1)}, u32[]{:S(2)}) copy-start(bf16[3584,128]{1,0:T(8,128)(2,1)} %copy-done.6) | copy-start | bytes 2752516
  217.1 63.9 %copy-start.5 = (bf16[3584,128]{1,0:T(8,128)(2,1)S(1)}, bf16[3584,128]{1,0:T(8,128)(2,1)}, u32[]{:S(2)}) copy-start(bf16[3584,128]{1,0:T(8,128)(2,1)} %copy-done.4) | copy-start | bytes 2752516
  217.1 65.0 %copy-start.3 = (bf16[3584,128]{1,0:T(8,128)(2,1)S(1)}, bf16[3584,128]{1,0:T(8,128)(2,1)}, u32[]{:S(2)}) copy-start(bf16[3584,128]{1,0:T(8,128)(2,1)} %copy-done.2) | copy-start | bytes 2752516
  219.2 66.0 %copy-start.26 = (bf16[2048,128]{1,0:T(8,128)(2,1)S(1)}, bf16[2048,128]{1,0:T(8,128)(2,1)}, u32[]{:S(2)}) copy-start(bf16[2048,128]{1,0:T(8,128)(2,1)} %param.9) | copy-start | bytes 1572868
  305.7 191.2 %reduce-scatter.4.cloned.1.call-start = ((), (), s32[]{:S(2)}) async-start(), calls=%async_computation.2 | async-start | bytes 15597568
  (12 other events, 11.3 us)
Sparse Core Ops, SparseCore 0:
  305.8 47.8 all-gather.5
  408.0 88.8 reduce-scatter.3
